TPU v7x, 32 devices: a whole 2x2x4 slice. The times are simulated.
32 devices in a mesh: tok: 4 (over y, core), tp: 8 (over z, x).
Axes of the slice: x: 2, y: 2, z: 4, core: 2. Of those that a mesh axis runs over, the one named last changes fastest.
Arguments:
- residual: bfloat16 [1024, 16384], P('tok', 'tp')
- norm_gain: float32 [16384], replicated, may hold values from 0.5 to 1.5
- weight: bfloat16 [30720, 16384], P(('tok', 'tp')), may hold values from -6 to 6
- scale_codes: int32 [30720, 2], P(('tok', 'tp')), may hold values from 0 to 7
- zero_points: int32 [30720, 2], P(('tok', 'tp')), may hold values from 4 to 11
- panels: bfloat16 [256, 16384], P(None, ('tok', 'tp')), as said below
Outputs:
- gram: float32 [16384, 16384], P('tok', 'tp')
- quantized: bfloat16 [30720, 16384], P('tok', 'tp')
Inputs may be any that keep to these rules, and one draw needn't show every extreme that they name: Row j of panels is row j of an upper-triangular factor: entries left of column j are zero and panels[j, j] lies in [0.5, 1.5].
All inputs are finite; a program needn't handle non-finite values.
Results may differ from a plain program's by a relative error of at most 0.0085.
Values may be sent and summed in bfloat16 or wider, within the bound.
A program may use at most 384 MiB of HBM per device.

v0:
```python
import math
import jax
import jax.numpy as jnp
from jax import lax
from jax.sharding import PartitionSpec as P

BLOCK = 128
BLOCKS = 2
EPS = 1e-05
SOFTNESS = 0.9
FULL_TURN = 2.0 * math.pi
HIGHEST = lax.Precision.HIGHEST


def spread(x, axis, root):
    mine = lax.axis_index(axis) == root
    return lax.psum(jnp.where(mine, x, jnp.zeros_like(x)), axis)


def dequantize(column, scale_row, zero_row):
    shifted = column / scale_row + zero_row
    softened = shifted - SOFTNESS * jnp.sin(FULL_TURN * shifted) / FULL_TURN
    return scale_row * (jnp.clip(softened, 0.0, 15.0) - zero_row)


def block_errors(block_cols, diagonal, scale_row, zero_row):
    row_count = block_cols.shape[0]
    block_width = block_cols.shape[1]
    lane_ids = lax.iota(jnp.int32, 8)
    wide_ids = lax.iota(jnp.int32, block_width)

    def sub_step(step_index, carried):
        block_now, errors = carried
        sub_first = step_index * 8
        sub_cols = lax.dynamic_slice_in_dim(block_now, sub_first, 8, 1)
        sub_panel = lax.dynamic_slice_in_dim(diagonal, sub_first, 8, 0)
        local_pivots = lax.dynamic_slice_in_dim(sub_panel, sub_first, 8, 1)
        collected = []
        for i in range(8):
            column_now = sub_cols[:, i]
            restored = dequantize(column_now, scale_row, zero_row)
            error_now = (column_now - restored) / local_pivots[i, i]
            sub_cols = (
                sub_cols
                - error_now[:, None] * jnp.where(lane_ids > i, local_pivots[i], 0.0)[None, :]
            )
            sub_cols = jnp.where((lane_ids == i)[None, :], restored[:, None], sub_cols)
            collected.append(error_now)
        sub_errors = jnp.stack(collected, axis=1)
        spill_over = jnp.dot(sub_errors, sub_panel, precision=HIGHEST)
        block_now = jnp.where(
            (wide_ids >= sub_first + 8)[None, :], block_now - spill_over, block_now
        )
        block_now = lax.dynamic_update_slice_in_dim(block_now, sub_cols, sub_first, 1)
        errors = lax.dynamic_update_slice_in_dim(errors, sub_errors, sub_first, 1)
        return (block_now, errors)

    start_state = (block_cols, jnp.zeros((row_count, block_width), jnp.float32))
    return lax.fori_loop(0, block_width // 8, sub_step, start_state)


def on_device(residual, norm_gain, weight, scale_codes, zero_points, panels):
    tok_local, feat_local = residual.shape
    tp_count = lax.axis_size("tp")
    tok_count = lax.axis_size("tok")
    feat_total = feat_local * tp_count
    tp_place = lax.axis_index("tp")
    local_rows = residual.astype(jnp.float32)
    row_sums = lax.psum(jnp.sum(local_rows * local_rows, axis=1), "tp")
    gain_own = lax.dynamic_slice_in_dim(norm_gain, tp_place * feat_local, feat_local, 0)
    x_own = (
        local_rows * lax.rsqrt(row_sums[:, None] / feat_total + EPS) * gain_own[None, :]
    ).astype(jnp.bfloat16)
    x_full = lax.all_gather(x_own, "tp", axis=1, tiled=True)
    gram_sum = lax.psum_scatter(
        lax.dot_general(
            x_full, x_own, (((0,), (0,)), ((), ())), preferred_element_type=jnp.float32
        ).astype(jnp.bfloat16),
        "tok",
        scatter_dimension=0,
        tiled=True,
    ).astype(jnp.float32)
    gram = gram_sum / (tok_local * tok_count)
    shard_cols = panels.shape[1]
    working = weight.astype(jnp.float32)
    column = lax.iota(jnp.int32, feat_total)
    for k in range(BLOCKS):
        block_start = k * BLOCK
        scale_row = jnp.exp2(scale_codes[:, k].astype(jnp.float32) * 0.5 - 3.0)
        zero_row = zero_points[:, k].astype(jnp.float32)
        root_index = block_start // shard_cols
        offset_cols = block_start - root_index * shard_cols
        own_block = panels[block_start : block_start + BLOCK, offset_cols : offset_cols + BLOCK]
        diagonal = spread(own_block, ("tok", "tp"), root_index).astype(jnp.float32)
        block_cols, errors = block_errors(
            working[:, block_start : block_start + BLOCK], diagonal, scale_row, zero_row
        )
        correction = jnp.dot(
            errors,
            lax.all_gather(
                panels[block_start : block_start + BLOCK], ("tok", "tp"), axis=1, tiled=True
            ).astype(jnp.float32),
            precision=HIGHEST,
        )
        working = jnp.where((column >= block_start + BLOCK)[None, :], working - correction, working)
        working = lax.dynamic_update_slice_in_dim(working, block_cols, block_start, 1)
    quantized = lax.all_to_all(
        working.astype(jnp.bfloat16), "tp", split_axis=1, concat_axis=0, tiled=True
    )
    return (gram, quantized)


def solution(mesh):
    in_specs = (
        P("tok", "tp"),
        P(),
        P(("tok", "tp"), None),
        P(("tok", "tp"), None),
        P(("tok", "tp"), None),
        P(None, ("tok", "tp")),
    )
    out_specs = (P("tok", "tp"), P("tok", "tp"))
    return jax.shard_map(
        on_device, mesh=mesh, in_specs=in_specs, out_specs=out_specs, check_vma=False
    )
```

profile of v0, /device:TPU:1, one launch (start us, length us, event | category | flops | bytes accessed | tf_op | source)
XLA Modules:
  0.0 1459.3 jit_solution(8556736024828552044)
XLA Ops:
  12.7 18.7 %psum.21 = f32[256]{0:T(256)S(1)} all-reduce(f32[256]{0:T(256)S(1)} %fusion.62), channel_id=1, replica_groups=mesh['tok'=4,'tp'=8] {'tp'}, use_global_device_ids=true, to_apply=%region_1.0 | all-reduce | flops 256 | bytes 2048 | tf_op jit(solution)/shard_map/psum | solution.py:69
  37.4 100.4 %all-reduce.4.cloned.1.call-done = (bf16[128,128]{1,0:T(8,128)(2,1)}, bf16[128,128]{1,0:T(8,128)(2,1)}) async-done(((bf16[128,128]{1,0:T(8,128)(2,1)}, bf16[128,128]{1,0:T(8,128)(2,1)}), (bf16[128,128]{1,0:T(8,128)(2,1)}, bf16[128,128]{1,0:T(8,128)(2,1)})) %all-reduce.4.cloned.1.call-update) | async-done | bytes 65552 | tf_op jit(solution)/shard_map/psum | solution.py:17
  138.6 221.0 %while.40 = (s32[]{:T(128)}, f32[960,128]{0,1:T(8,128)S(1)}, f32[960,128]{0,1:T(8,128)S(1)}, f32[960]{0:T(1024)S(1)}, f32[960]{0:T(1024)S(1)}, /*index=5*/f32[12...) while((s32[]{:T(128)}, f32[960,128]{0,1:T(8,128)S(1)}, ...), condition=%wide.region_5.6_spmd.clone.clone, body=%wide.region_4.5_spmd.clone.clone.sunk | while | flops 12948808 | bytes 4160943 | solution.py:59
  160.8 4.5 dynamic_update_slice.69
  174.6 4.5 dynamic_update_slice.69
  188.5 4.5 dynamic_update_slice.69
  202.4 4.5 dynamic_update_slice.69
  216.2 4.5 dynamic_update_slice.69
  230.1 4.5 dynamic_update_slice.69
  244.0 4.5 dynamic_update_slice.69
  257.8 4.5 dynamic_update_slice.69
  271.7 4.5 dynamic_update_slice.69
  285.5 4.5 dynamic_update_slice.69
  313.3 4.5 dynamic_update_slice.69
  327.1 4.5 dynamic_update_slice.69
  354.8 4.5 dynamic_update_slice.69
  360.5 42.3 %subtract_select_fusion.17 = f32[960,16384]{1,0:T(8,128)} fusion(f32[960,128]{0,1:T(8,128)S(1)} %get-tuple-element.574, bf16[128,16384]{1,0:T(8,128)(2,1)} %all-gather.6.cloned.1.call-done, pred[16384]{0:T(1024)(128)(4,1)S(1)} %iota_compare_fusion.34, bf16[960,16384]{1,0:T(8,128)(2,1)} %param.12), kind=kOutput, calls=%fused_computation.145 | convolution fusion | flops 24206376960 | bytes 99074048 | tf_op jit(solution)/shard_map/dot_general | solution.py:98
  405.0 29.4 %convolution_convert_fusion = bf16[16384,2048]{1,0:T(8,128)(2,1)} fusion(bf16[256,16384]{1,0:T(8,128)(2,1)} %all-gather.4.cloned.1.call-done, bf16[256,2048]{1,0:T(8,128)(2,1)S(1)} %copy-done), kind=kOutput, calls=%fused_computation.146 | convolution fusion | flops 17213423616 | bytes 76546048 | tf_op jit(solution)/shard_map/dot_general | solution.py:76
  434.5 226.1 %while.41 = (s32[]{:T(128)}, f32[960,128]{0,1:T(8,128)S(1)}, f32[960,128]{0,1:T(8,128)S(1)}, f32[960]{0:T(1024)S(1)}, f32[960]{0:T(1024)S(1)}, /*index=5*/f32[12...) while((s32[]{:T(128)}, f32[960,128]{0,1:T(8,128)S(1)}, ...), condition=%wide.region_8.9_spmd.clone.clone, body=%wide.region_7.8_spmd.clone.clone.sunk | while | flops 12948808 | bytes 4160943 | solution.py:59
  471.7 4.5 dynamic_update_slice.71
  485.9 4.5 dynamic_update_slice.71
  514.2 4.5 dynamic_update_slice.71
  556.7 4.5 dynamic_update_slice.71
  570.9 4.5 dynamic_update_slice.71
  585.1 4.5 dynamic_update_slice.71
  599.2 4.5 dynamic_update_slice.71
  655.9 4.5 dynamic_update_slice.71
  660.8 41.6 %subtract_select_fusion.16 = bf16[960,16384]{1,0:T(8,128)(2,1)} fusion(f32[960,16384]{1,0:T(8,128)} %constant_dynamic-update-slice_fusion.3, f32[960,128]{0,1:T(8,128)S(1)} %get-tuple-element.576, bf16[128,16384]{1,0:T(8,128)(2,1)} %all-gather.8.cloned.1.call-done, pred[16384]{0:T(1024)(128)(4,1)S(1)} %iota_compare_fusion.35), kind=kOutput, calls=%fused_computation.144 | convolution fusion | flops 24190648320 | bytes 99074048 | tf_op jit(solution)/shard_map/dot_general | solution.py:98
  703.2 21.7 %copy.170 = bf16[120,8,8,2048]{3,2,0,1:T(8,128)(2,1)} copy(bf16[120,8,8,2048]{3,2,1,0:T(8,128)(2,1)} %bitcast.316) | data formatting | bytes 62914560 | tf_op jit(solution)/shard_map/all_to_all | solution.py:107
  724.9 687.8 %all_to_all.19 = bf16[960,8,2048]{2,0,1:T(8,128)(2,1)} all-to-all(bf16[960,8,2048]{2,0,1:T(8,128)(2,1)} %bitcast.318), channel_id=1, replica_groups=mesh['tok'=4,'tp'=8] {'tp'}, dimensions={1} | all-to-all | bytes 62914560 | tf_op jit(solution)/shard_map/all_to_all | solution.py:107
  1412.6 18.8 %convert_multiply_fusion = f32[4096,2048]{1,0:T(8,128)} fusion(bf16[4096,2048]{1,0:T(8,128)(2,1)} %reduce-scatter.4.cloned.1.call-done), kind=kLoop, calls=%fused_computation.147 | loop fusion | flops 16777216 | bytes 50331648 | tf_op jit(solution)/shard_map/div | solution.py:83
  1431.4 21.3 %copy.210 = bf16[7680,2048]{1,0:T(8,128)(2,1)} copy(bf16[7680,2048]{1,0:T(8,128)(2,1)} %bitcast.317) | data formatting | bytes 62914560
  (1137 shorter events, 363.9 us)
Async XLA Ops:
  7.2 130.6 %all-reduce.4.cloned.1.call-start = ((), (), s32[]{:S(2)}) async-start(), calls=%async_computation.6 | async-start | bytes 131072 | tf_op jit(solution)/shard_map/psum | solution.py:17
  8.7 351.9 %all-gather.6.cloned.1.call-start = ((), (), s32[]{:S(2)}) async-start(), calls=%async_computation.3 | async-start | bytes 4325376 | tf_op jit(solution)/shard_map/all_gather | solution.py:100
  10.4 394.6 %all-gather.4.cloned.1.call-start = ((), (), s32[]{:S(2)}) async-start(), calls=%async_computation.2 | async-start | bytes 9437184 | tf_op jit(solution)/shard_map/all_gather | solution.py:74
  33.9 626.9 %all-gather.8.cloned.1.call-start = ((), (), s32[]{:S(2)}) async-start(), calls=%async_computation.4 | async-start | bytes 4325376 | tf_op jit(solution)/shard_map/all_gather | solution.py:100
  34.5 1378.1 %reduce-scatter.4.cloned.1.call-start = ((), (), s32[]{:S(2)}) async-start(), calls=%async_computation.5 | async-start | bytes 83886080
  360.5 44.5 %copy-start = (bf16[256,2048]{1,0:T(8,128)(2,1)S(1)}, bf16[256,2048]{1,0:T(8,128)(2,1)}, u32[]{:S(2)}) copy-start(bf16[256,2048]{1,0:T(8,128)(2,1)} %fusion.64) | copy-start | bytes 3145732
Sparse Core Ops, SparseCore 0:
  13.7 124.0 all-reduce.3
  140.6 62.9 all-gather.5
  206.4 121.5 all-gather.3
  331.3 62.2 all-gather.7
  434.5 445.9 reduce-scatter.3
where the time goes:
time: 1460 us
  blocking collectives  706 us (48%)
  other arithmetic  251 us (17%)
  local copies, waits for them, and re-layouts  237 us (16%)
  matrix products  144 us (10%)
  waiting for transfers between devices  101 us (7%)
    all_to_all x1, blocking collectives, on_device(): lax.all_to_all(working.astype(jnp.bfloat16), 'tp', split_axis=1, concat_a...  688 us
    div x256, other arithmetic, sub_step(): error_now = (column_now - restored) / local_pivots[i, i]  197 us
    dynamic_update_slice x32, local copies, waits for them, and re-layouts, sub_step(): lax.dynamic_update_slice_in_dim(block_now, sub_cols, sub_first, 1)  142 us
    psum x1, waiting for transfers between devices, spread(): return lax.psum(jnp.where(mine, x, jnp.zeros_like(x)), axis)  100 us
    dot_general x2, matrix products, on_device(): jnp.dot(errors, lax.all_gather(panels[block_start:block_start + BLOCK], (...  84 us
    dot_general x32, matrix products, sub_step(): spill_over = jnp.dot(sub_errors, sub_panel, precision=HIGHEST)  30.6 us
    dot_general x1, matrix products, on_device(): lax.dot_general(x_full, x_own, (((0,), (0,)), ((), ())), preferred_elemen...  29.4 us
  transfers between devices with their start and end apart: 5, of which 1 were waited for; matrix products, arithmetic and copies ran while one was open for 40% of the time, Pallas kernels for 0%

commit v1 on v0

--- a/solution.py
+++ b/solution.py
@@ -104,9 +104,20 @@
         )
         working = jnp.where((column >= block_start + BLOCK)[None, :], working - correction, working)
         working = lax.dynamic_update_slice_in_dim(working, block_cols, block_start, 1)
-    quantized = lax.all_to_all(
-        working.astype(jnp.bfloat16), "tp", split_axis=1, concat_axis=0, tiled=True
-    )
+    x_2 = working.astype(jnp.bfloat16)
+    ways, here = (lax.axis_size("tp"), lax.axis_index("tp"))
+    width = x_2.shape[1] // ways
+    shape = list(x_2.shape)
+    shape[1] = width
+    height = shape[0]
+    shape[0] = height * ways
+    full = jnp.zeros(shape, x_2.dtype)
+    for mask in range(ways):
+        part = lax.dynamic_slice_in_dim(x_2, (here ^ mask) * width, width, axis=1)
+        if mask:
+            part = lax.ppermute(part, "tp", [(d, d ^ mask) for d in range(ways)])
+        full = lax.dynamic_update_slice_in_dim(full, part, (here ^ mask) * height, axis=0)
+    quantized = full
     return (gram, quantized)
 
 

time: 1460 us -> 1540 us (1.055)
  the two profiles are of different devices: /device:TPU:1 before, /device:TPU:22 now
where the time goes in v1:
time: 1540 us
  waiting for transfers between devices  838 us (54%)
  local copies, waits for them, and re-layouts  255 us (17%)
  other arithmetic  254 us (16%)
  matrix products  142 us (9%)
  between operations  15.9 us (1%)
    ppermute x7, waiting for transfers between devices, on_device(): part = lax.ppermute(part, 'tp', [(d, d ^ mask) for d in range(ways)])  644 us
    div x256, other arithmetic, sub_step(): error_now = (column_now - restored) / local_pivots[i, i]  200 us
    psum x1, waiting for transfers between devices, spread(): return lax.psum(jnp.where(mine, x, jnp.zeros_like(x)), axis)  193 us
    dynamic_update_slice x32, local copies, waits for them, and re-layouts, sub_step(): lax.dynamic_update_slice_in_dim(block_now, sub_cols, sub_first, 1)  142 us
    dot_general x2, matrix products, on_device(): jnp.dot(errors, lax.all_gather(panels[block_start:block_start + BLOCK], (...  83.1 us
    dynamic_update_slice x7, local copies, waits for them, and re-layouts, on_device(): lax.dynamic_update_slice_in_dim(full, part, (here ^ mask) * height, axis=0)  32 us
  transfers between devices with their start and end apart: 12, of which 7 were waited for; matrix products, arithmetic and copies ran while one was open for 41% of the time, Pallas kernels for 0%

profile of v1, /device:TPU:22, one launch (start us, length us, event | category | flops | bytes accessed | tf_op | source)
XLA Modules:
  0.0 1536.6 jit_solution(2993332015918634205)
XLA Ops:
  11.0 15.2 psum.21
  34.8 193.4 %all-reduce.4.cloned.1.call-done = (bf16[128,128]{1,0:T(8,128)(2,1)}, bf16[128,128]{1,0:T(8,128)(2,1)}) async-done(((bf16[128,128]{1,0:T(8,128)(2,1)}, bf16[128,128]{1,0:T(8,128)(2,1)}), (bf16[128,128]{1,0:T(8,128)(2,1)}, bf16[128,128]{1,0:T(8,128)(2,1)})) %all-reduce.4.cloned.1.call-update) | async-done | bytes 65552 | tf_op jit(solution)/shard_map/psum | solution.py:17
  228.9 28.4 %convolution_convert_fusion = bf16[16384,2048]{1,0:T(8,128)(2,1)} fusion(bf16[256,16384]{1,0:T(8,128)(2,1)} %all-gather.4.cloned.1.call-done, bf16[256,2048]{1,0:T(8,128)(2,1)} %fusion.64), kind=kOutput, calls=%fused_computation.146 | convolution fusion | flops 17213423616 | bytes 76546048 | tf_op jit(solution)/shard_map/dot_general | solution.py:76
  257.4 223.7 %while.40 = (s32[]{:T(128)}, f32[960,128]{0,1:T(8,128)S(1)}, f32[960,128]{0,1:T(8,128)S(1)}, f32[960]{0:T(1024)S(1)}, f32[960]{0:T(1024)S(1)}, /*index=5*/f32[12...) while((s32[]{:T(128)}, f32[960,128]{0,1:T(8,128)S(1)}, ...), condition=%wide.region_5.6_spmd.clone.clone, body=%wide.region_4.5_spmd.clone.clone.sunk | while | flops 12948808 | bytes 4160943 | solution.py:59
  280.0 4.5 dynamic_update_slice.109
  294.0 4.5 dynamic_update_slice.109
  322.1 4.5 dynamic_update_slice.109
  392.3 4.5 dynamic_update_slice.109
  448.4 4.5 dynamic_update_slice.109
  462.4 4.5 dynamic_update_slice.109
  476.4 4.5 dynamic_update_slice.109
  481.4 42.4 %subtract_select_fusion.17 = f32[960,16384]{1,0:T(8,128)} fusion(f32[960,128]{0,1:T(8,128)S(1)} %get-tuple-element.574, bf16[128,16384]{1,0:T(8,128)(2,1)} %all-gather.6.cloned.1.call-done, pred[16384]{0:T(1024)(128)(4,1)S(1)} %iota_compare_fusion.34, bf16[960,16384]{1,0:T(8,128)(2,1)} %param.12), kind=kOutput, calls=%fused_computation.145 | convolution fusion | flops 24206376960 | bytes 99074048 | tf_op jit(solution)/shard_map/dot_general | solution.py:98
  526.1 225.6 %while.41 = (s32[]{:T(128)}, f32[960,128]{0,1:T(8,128)S(1)}, f32[960,128]{0,1:T(8,128)S(1)}, f32[960]{0:T(1024)S(1)}, f32[960]{0:T(1024)S(1)}, /*index=5*/f32[12...) while((s32[]{:T(128)}, f32[960,128]{0,1:T(8,128)S(1)}, ...), condition=%wide.region_8.9_spmd.clone.clone, body=%wide.region_7.8_spmd.clone.clone.sunk | while | flops 12948808 | bytes 4160943 | solution.py:59
  549.0 4.5 dynamic_update_slice.111
  563.2 4.5 dynamic_update_slice.111
  751.9 40.7 %subtract_select_fusion.16 = bf16[960,16384]{1,0:T(8,128)(2,1)} fusion(f32[960,16384]{1,0:T(8,128)} %constant_dynamic-update-slice_fusion.10, f32[960,128]{0,1:T(8,128)S(1)} %get-tuple-element.576, bf16[128,16384]{1,0:T(8,128)(2,1)} %all-gather.8.cloned.1.call-done, pred[16384]{0:T(1024)(128)(4,1)S(1)} %iota_compare_fusion.35), kind=kOutput, calls=%fused_computation.144 | convolution fusion | flops 24190648320 | bytes 99074048 | tf_op jit(solution)/shard_map/dot_general | solution.py:98
  793.3 10.5 broadcast_in_dim.980
  803.9 19.6 %constant_dynamic-slice_fusion = (bf16[960,2048]{1,0:T(8,128)(2,1)}, bf16[960,2048]{1,0:T(8,128)(2,1)}, bf16[960,2048]{1,0:T(8,128)(2,1)}, bf16[960,2048]{1,0:T(...) fusion(bf16[960,16384]{1,0:T(8,128)(2,1)} %constant_dynamic-upd, ...), kind=kLoop, calls=%fused_computation.158 | loop fusion | bytes 62914596 | tf_op jit(solution)/shard_map/dynamic_slice | solution.py:116
  832.0 77.5 %collective-permute-done = bf16[960,2048]{1,0:T(8,128)(2,1)} collective-permute-done((bf16[960,2048]{1,0:T(8,128)(2,1)S(1)}, bf16[960,2048]{1,0:T(8,128)(2,1)}, u32[]{:S(2)}, u32[]{:S(2)}) %collective-permute-start) | collective-permute-done | bytes 3932192 | tf_op jit(solution)/shard_map/ppermute | solution.py:118
  911.4 166.0 %collective-permute-done.1 = bf16[960,2048]{1,0:T(8,128)(2,1)} collective-permute-done((bf16[960,2048]{1,0:T(8,128)(2,1)S(1)}, bf16[960,2048]{1,0:T(8,128)(2,1)}, u32[]{:S(2)}, u32[]{:S(2)}) %collective-permute-start.1) | collective-permute-done | bytes 3932192 | tf_op jit(solution)/shard_map/ppermute | solution.py:118
  1077.4 4.6 constant_dynamic-update-slice_fusion.7
  1082.0 4.6 constant_dynamic-update-slice_fusion.6
  1086.6 74.8 %collective-permute-done.2 = bf16[960,2048]{1,0:T(8,128)(2,1)} collective-permute-done((bf16[960,2048]{1,0:T(8,128)(2,1)}, bf16[960,2048]{1,0:T(8,128)(2,1)}, u32[]{:S(2)}, u32[]{:S(2)}) %collective-permute-start.2) | collective-permute-done | bytes 3932192 | tf_op jit(solution)/shard_map/ppermute | solution.py:118
  1161.4 4.6 constant_dynamic-update-slice_fusion.5
  1166.0 4.6 constant_dynamic-update-slice_fusion.4
  1170.6 164.4 %collective-permute-done.4 = bf16[960,2048]{1,0:T(8,128)(2,1)} collective-permute-done((bf16[960,2048]{1,0:T(8,128)(2,1)}, bf16[960,2048]{1,0:T(8,128)(2,1)}, u32[]{:S(2)}, u32[]{:S(2)}) %collective-permute-start.4) | collective-permute-done | bytes 3932192 | tf_op jit(solution)/shard_map/ppermute | solution.py:118
  1335.0 4.6 constant_dynamic-update-slice_fusion.3
  1339.5 81.8 %collective-permute-done.5 = bf16[960,2048]{1,0:T(8,128)(2,1)} collective-permute-done((bf16[960,2048]{1,0:T(8,128)(2,1)}, bf16[960,2048]{1,0:T(8,128)(2,1)}, u32[]{:S(2)}, u32[]{:S(2)}) %collective-permute-start.5) | collective-permute-done | bytes 3932192 | tf_op jit(solution)/shard_map/ppermute | solution.py:118
  1421.3 4.6 constant_dynamic-update-slice_fusion.2
  1425.9 79.7 %collective-permute-done.6 = bf16[960,2048]{1,0:T(8,128)(2,1)} collective-permute-done((bf16[960,2048]{1,0:T(8,128)(2,1)}, bf16[960,2048]{1,0:T(8,128)(2,1)}, u32[]{:S(2)}, u32[]{:S(2)}) %collective-permute-start.6) | collective-permute-done | bytes 3932192 | tf_op jit(solution)/shard_map/ppermute | solution.py:118
  1505.6 4.6 constant_dynamic-update-slice_fusion.8
  1510.2 18.8 %convert_multiply_fusion = f32[4096,2048]{1,0:T(8,128)} fusion(bf16[4096,2048]{1,0:T(8,128)(2,1)} %reduce-scatter.4.cloned.1.call-done), kind=kLoop, calls=%fused_computation.147 | loop fusion | flops 16777216 | bytes 50331648 | tf_op jit(solution)/shard_map/div | solution.py:83
  (1157 shorter events, 429.5 us)
Async XLA Ops:
  8.0 220.2 %all-reduce.4.cloned.1.call-start = ((), (), s32[]{:S(2)}) async-start(), calls=%async_computation.5 | async-start | bytes 131072 | tf_op jit(solution)/shard_map/psum | solution.py:17
  9.5 219.5 %all-gather.4.cloned.1.call-start = ((), (), s32[]{:S(2)}) async-start(), calls=%async_computation.1 | async-start | bytes 9437184 | tf_op jit(solution)/shard_map/all_gather | solution.py:74
  29.5 451.9 %all-gather.6.cloned.1.call-start = ((), (), s32[]{:S(2)}) async-start(), calls=%async_computation.2 | async-start | bytes 4325376 | tf_op jit(solution)/shard_map/all_gather | solution.py:100
  31.2 720.7 %all-gather.8.cloned.1.call-start = ((), (), s32[]{:S(2)}) async-start(), calls=%async_computation.3 | async-start | bytes 4325376 | tf_op jit(solution)/shard_map/all_gather | solution.py:100
  31.8 1478.4 %reduce-scatter.4.cloned.1.call-start = ((), (), s32[]{:S(2)}) async-start(), calls=%async_computation.4 | async-start | bytes 83886080
  257.4 224.0 %copy-start = (bf16[128,128]{1,0:T(8,128)(2,1)S(1)}, bf16[128,128]{1,0:T(8,128)(2,1)}, u32[]{:S(2)}) copy-start(bf16[128,128]{1,0:T(8,128)(2,1)} %get-tuple-element.725) | copy-start | bytes 98308
  823.4 86.1 %collective-permute-start = (bf16[960,2048]{1,0:T(8,128)(2,1)S(1)}, bf16[960,2048]{1,0:T(8,128)(2,1)}, u32[]{:S(2)}, u32[]{:S(2)}) collective-permute-start(bf16[960,2048]{1,0:T(8,128)(2,1)S(1)} %get-tuple-element.796), channel_id=1, source_target_pairs={{0,1},{1,0},{2,3},{3,2},{4,5},{5,4},{6,7},{7,6},{8,9},{9,8},{10,11... | collective-permute-start | bytes 11796488 | tf_op jit(solution)/shard_map/ppermute | solution.py:118
  826.1 251.3 %collective-permute-start.1 = (bf16[960,2048]{1,0:T(8,128)(2,1)S(1)}, bf16[960,2048]{1,0:T(8,128)(2,1)}, u32[]{:S(2)}, u32[]{:S(2)}) collective-permute-start(bf16[960,2048]{1,0:T(8,128)(2,1)S(1)} %get-tuple-element.795), channel_id=1, source_target_pairs={{0,2},{1,3},{2,0},{3,1},{4,6},{5,7},{6,4},{7,5},{8,10},{9,11},{10,... | collective-permute-start | bytes 11796488 | tf_op jit(solution)/shard_map/ppermute | solution.py:118
  826.1 335.3 %collective-permute-start.2 = (bf16[960,2048]{1,0:T(8,128)(2,1)}, bf16[960,2048]{1,0:T(8,128)(2,1)}, u32[]{:S(2)}, u32[]{:S(2)}) collective-permute-start(bf16[960,2048]{1,0:T(8,128)(2,1)} %get-tuple-element.794), channel_id=1, source_target_pairs={{0,3},{1,2},{2,1},{3,0},{4,7},{5,6},{6,5},{7,4},{8,11},{9,10},{10,... | collective-permute-start | bytes 11796488 | tf_op jit(solution)/shard_map/ppermute | solution.py:118
  827.7 338.3 %collective-permute-start.3 = (bf16[960,2048]{1,0:T(8,128)(2,1)}, bf16[960,2048]{1,0:T(8,128)(2,1)}, u32[]{:S(2)}, u32[]{:S(2)}) collective-permute-start(bf16[960,2048]{1,0:T(8,128)(2,1)} %get-tuple-element.793), channel_id=1, source_target_pairs={{0,4},{1,5},{2,6},{3,7},{4,0},{5,1},{6,2},{7,3},{8,12},{9,13},{10,... | collective-permute-start | bytes 11796488 | tf_op jit(solution)/shard_map/ppermute | solution.py:118
  828.0 507.0 %collective-permute-start.4 = (bf16[960,2048]{1,0:T(8,128)(2,1)}, bf16[960,2048]{1,0:T(8,128)(2,1)}, u32[]{:S(2)}, u32[]{:S(2)}) collective-permute-start(bf16[960,2048]{1,0:T(8,128)(2,1)} %get-tuple-element.792), channel_id=1, source_target_pairs={{0,5},{1,4},{2,7},{3,6},{4,1},{5,0},{6,3},{7,2},{8,13},{9,12},{10,... | collective-permute-start | bytes 11796488 | tf_op jit(solution)/shard_map/ppermute | solution.py:118
  909.5 511.8 %collective-permute-start.5 = (bf16[960,2048]{1,0:T(8,128)(2,1)}, bf16[960,2048]{1,0:T(8,128)(2,1)}, u32[]{:S(2)}, u32[]{:S(2)}) collective-permute-start(bf16[960,2048]{1,0:T(8,128)(2,1)} %get-tuple-element.791), channel_id=1, source_target_pairs={{0,6},{1,7},{2,4},{3,5},{4,2},{5,3},{6,0},{7,1},{8,14},{9,15},{10,... | collective-permute-start | bytes 11796488 | tf_op jit(solution)/shard_map/ppermute | solution.py:118
  1077.4 428.2 %collective-permute-start.6 = (bf16[960,2048]{1,0:T(8,128)(2,1)}, bf16[960,2048]{1,0:T(8,128)(2,1)}, u32[]{:S(2)}, u32[]{:S(2)}) collective-permute-start(bf16[960,2048]{1,0:T(8,128)(2,1)} %get-tuple-element.790), channel_id=1, source_target_pairs={{0,7},{1,6},{2,5},{3,4},{4,3},{5,2},{6,1},{7,0},{8,15},{9,14},{10,... | collective-permute-start | bytes 11796488 | tf_op jit(solution)/shard_map/ppermute | solution.py:118
Sparse Core Ops, SparseCore 0:
  14.5 213.6 all-reduce.3
Sparse Core Ops, SparseCore 1:
  29.6 126.3 all-gather.3
  158.7 61.1 all-gather.5
  223.2 61.0 all-gather.7
  286.9 445.8 reduce-scatter.3
